TPU v7x, 128 devices: a whole 4x4x4 slice. The times are simulated.
128 devices in a mesh: ctx: 32 (over y, z, core), head: 4 (over x).
Axes of the slice: x: 4, y: 4, z: 4, core: 2. Of those that a mesh axis runs over, the one named last changes fastest.
Arguments:
- stream: bfloat16 [16384, 2048], P(('ctx', 'head')), may hold values from -6 to 6
- moe_gain: float32 [2048], replicated, may hold values from 0.5 to 1.5
- router: bfloat16 [2048, 256], replicated, may hold values from -0.125 to 0.125
- expert_ids: int32 [16384, 10], P(('ctx', 'head')), may hold values from 0 to 255, all different within a row; in each aligned block of 128 rows (0 to 127, 128 to 255, ...) at most 6 rows name the same one
- expert_gate: bfloat16 [256, 2048, 512], P(('ctx', 'head')), may hold values from -0.125 to 0.125
- expert_up: bfloat16 [256, 2048, 512], P(('ctx', 'head')), may hold values from -0.125 to 0.125
- expert_down: bfloat16 [256, 512, 2048], P(('ctx', 'head')), may hold values from -1 to 1
- mixer_gain: float32 [2048], replicated, may hold values from 0.5 to 1.5
- query_weight: bfloat16 [2048, 1024], P(None, 'head'), may hold values from -0.125 to 0.125
- key_weight: bfloat16 [2048, 1024], P(None, 'head'), may hold values from -0.125 to 0.125
- value_weight: bfloat16 [2048, 2048], P(None, 'head'), may hold values from -0.125 to 0.125
- output_gate: bfloat16 [2048, 2048], P(None, 'head'), may hold values from -0.125 to 0.125
- beta_weight: bfloat16 [2048, 16], P(None, 'head'), may hold values from -0.125 to 0.125
- decay_weight: bfloat16 [2048, 16], P(None, 'head'), may hold values from -0.5 to 0.5
- query_conv: float32 [4, 1024], P(None, 'head'), may hold values from -3 to 3
- key_conv: float32 [4, 1024], P(None, 'head'), may hold values from -3 to 3
- value_conv: float32 [4, 2048], P(None, 'head'), may hold values from -3 to 3
- decay_log: float32 [16], P('head'), may hold values from -12 to -2.5
- decay_bias: float32 [16], P('head'), may hold values from -2 to 1
- head_gain: float32 [128], replicated, may hold values from 0.5 to 1.5
- out_weight: bfloat16 [2048, 2048], P('head'), may hold values from -0.125 to 0.125
Outputs:
- moe_out: bfloat16 [16384, 2048], P(('ctx', 'head'))
- mixer_out: bfloat16 [16384, 2048], P(('ctx', 'head'))
Inputs may be any that keep to these rules, and one draw needn't show every extreme that they name: `expert_ids`: each row names 10 different experts; in each aligned block of 128 rows (the rows of one device) no expert is named by more than 6 rows, a bound that some block reaches.
All inputs are finite; a program needn't handle non-finite values.
Results may differ from a plain program's by a relative error of at most 0.017.
Values may be sent and summed in bfloat16 or wider, within the bound.
A program may use at most 128 MiB of HBM per device.

v0:
```python
import math
import jax
import jax.numpy as jnp
from jax import lax
from jax.sharding import PartitionSpec as P

DK = 128
epsilon = 1e-06
exact_precision = lax.Precision.HIGHEST


def passed_along(value, axis, steps):
    count = lax.axis_size(axis)
    first, last = (max(0, -steps), min(count, count - steps))
    return lax.ppermute(value, axis, [(source, source + steps) for source in range(first, last)])


def prefix(array, axis, combine, identity):
    peers, place = (lax.axis_size(axis), lax.axis_index(axis))
    everything = jax.tree.map(
        lambda part, kind: lax.all_gather(part.astype(kind), axis),
        array,
        (jnp.bfloat16, jnp.bfloat16),
    )
    start = jax.tree.map(
        lambda part, zero: jnp.broadcast_to(jnp.asarray(zero, part.dtype), part.shape),
        array,
        identity,
    )

    def step(k, before):
        reached = k < place
        new = combine(
            before, jax.tree.map(lambda part, own: part[k].astype(own.dtype), everything, array)
        )
        return jax.tree.map(lambda a, b: jnp.where(reached, a, b), new, before)

    return lax.fori_loop(0, peers, step, start)


def rms_rows(values, gain):
    values = values.astype(jnp.float32)
    scale = lax.rsqrt(jnp.mean(values * values, axis=-1, keepdims=True) + epsilon)
    return values * scale * gain


def block_terms(queries, key_rows, values, strength, decays):
    length = queries.shape[0]
    cumulative = jnp.cumsum(decays)
    spread = cumulative[:, None] - cumulative[None, :]
    positions = jnp.arange(length, dtype=jnp.int32)
    strict = positions[:, None] > positions[None, :]
    inclusive = positions[:, None] >= positions[None, :]
    fall_strict = jnp.where(strict, jnp.exp(jnp.where(strict, spread, 0.0)), 0.0)
    fall_inclusive = jnp.where(inclusive, jnp.exp(jnp.where(inclusive, spread, 0.0)), 0.0)
    key_dots = jnp.dot(key_rows, key_rows.T, precision=exact_precision)
    strict_part = strength[:, None] * fall_strict * key_dots
    system = jnp.eye(length, dtype=jnp.float32) + strict_part
    targets = strength[:, None] * jnp.concatenate(
        [values, jnp.exp(cumulative)[:, None] * key_rows], axis=1
    )
    solved = jax.scipy.linalg.solve_triangular(system, targets, lower=True, unit_diagonal=True)
    value_width = values.shape[1]
    w_values = solved[:, :value_width]
    w_keys = solved[:, value_width:]
    mixing = fall_inclusive * jnp.dot(queries, key_rows.T, precision=exact_precision)
    q_decayed = jnp.exp(cumulative)[:, None] * queries
    k_decayed = jnp.exp(cumulative[-1] - cumulative)[:, None] * key_rows
    closing = jnp.exp(cumulative[-1])
    return (w_values, w_keys, mixing, q_decayed, k_decayed, closing)


def local_pass(queries, key_rows, values, strength, decays):
    length = queries.shape[0]
    block_len = math.gcd(length, 64)
    block_count = length // block_len

    def split_blocks(array):
        return array.reshape((block_count, block_len) + array.shape[1:])

    terms = jax.vmap(block_terms)(
        split_blocks(queries),
        split_blocks(key_rows),
        split_blocks(values),
        split_blocks(strength),
        split_blocks(decays),
    )

    def advance(carried_pair, block_term):
        state_now, transfer = carried_pair
        w_values, w_keys, mixing, q_decayed, k_decayed, closing = block_term
        update = w_values - jnp.dot(w_keys, state_now, precision=exact_precision)
        result = jnp.dot(q_decayed, state_now, precision=exact_precision) + jnp.dot(
            mixing, update, precision=exact_precision
        )
        moved_rows = jnp.dot(w_keys, transfer, precision=exact_precision)
        reading = jnp.dot(q_decayed, transfer, precision=exact_precision) - jnp.dot(
            mixing, moved_rows, precision=exact_precision
        )
        state_now = closing * state_now + jnp.dot(k_decayed.T, update, precision=exact_precision)
        transfer = closing * transfer - jnp.dot(k_decayed.T, moved_rows, precision=exact_precision)
        return ((state_now, transfer), (result, reading))

    key_width = key_rows.shape[1]
    initial = (
        jnp.zeros((key_width, values.shape[1]), jnp.float32),
        jnp.eye(key_width, dtype=jnp.float32),
    )
    (state_now, transfer), (results, read_values) = lax.scan(advance, initial, terms)
    return (results.reshape(length, -1), read_values.reshape(length, -1), transfer, state_now)


def unit_heads(array, heads):
    reshaped_rows = array.reshape(array.shape[0], heads, -1)
    return reshaped_rows * lax.rsqrt(
        jnp.sum(reshaped_rows * reshaped_rows, axis=-1, keepdims=True) + epsilon
    )


def on_device(
    stream,
    moe_gain,
    router,
    expert_ids,
    expert_gate,
    expert_up,
    expert_down,
    mixer_gain,
    query_weight,
    key_weight,
    value_weight,
    output_gate,
    beta_weight,
    decay_weight,
    query_conv,
    key_conv,
    value_conv,
    decay_log,
    decay_bias,
    head_gain,
    out_weight,
):
    ctx_count = lax.axis_size("ctx")
    head_count = lax.axis_size("head")
    sources = ctx_count * head_count
    tok_rows, model_width = stream.shape
    top_count = expert_ids.shape[1]
    local_experts = expert_gate.shape[0]
    experts_all = local_experts * sources
    capacity = (11 * tok_rows * top_count + 10 * experts_all - 1) // (10 * experts_all)
    normed = rms_rows(stream, moe_gain).astype(jnp.bfloat16)
    logits = jnp.dot(normed, router, preferred_element_type=jnp.float32)
    chosen = jnp.take_along_axis(logits, expert_ids, axis=1)
    raised = jnp.exp(chosen)
    weights = raised / jnp.sum(raised, axis=1, keepdims=True)
    flat_ids = expert_ids.reshape(-1)
    matches = (flat_ids[:, None] == jnp.arange(experts_all, dtype=jnp.int32)[None, :]).astype(
        jnp.int32
    )
    slot_index = jnp.sum((jnp.cumsum(matches, axis=0) - 1) * matches, axis=1)
    places = flat_ids * capacity + slot_index
    token_rows = jnp.arange(tok_rows * top_count, dtype=jnp.int32) // top_count
    outgoing = (
        jnp.zeros((experts_all * capacity, model_width), jnp.bfloat16)
        .at[places]
        .set(normed[token_rows])
    )
    outgoing = outgoing.reshape(sources, local_experts, capacity, model_width)
    received = lax.all_to_all(outgoing, ("ctx", "head"), split_axis=0, concat_axis=0, tiled=True)
    gate_part = jnp.einsum(
        "nesd,edh->nesh", received, expert_gate, preferred_element_type=jnp.float32
    )
    up_part = jnp.einsum("nesd,edh->nesh", received, expert_up, preferred_element_type=jnp.float32)
    hidden = (jax.nn.silu(gate_part) * up_part).astype(jnp.bfloat16)
    returned = lax.all_to_all(
        jnp.einsum(
            "nesh,ehd->nesd", hidden, expert_down, preferred_element_type=jnp.float32
        ).astype(jnp.bfloat16),
        ("ctx", "head"),
        split_axis=0,
        concat_axis=0,
        tiled=True,
    )
    gathered_rows = returned.reshape(experts_all * capacity, model_width)[places].reshape(
        tok_rows, top_count, model_width
    )
    moe_out = jnp.sum(weights[:, :, None] * gathered_rows.astype(jnp.float32), axis=1).astype(
        jnp.bfloat16
    )
    mixer_in = rms_rows(
        stream.astype(jnp.float32) + moe_out.astype(jnp.float32), mixer_gain
    ).astype(jnp.bfloat16)
    weight_list = (query_weight, key_weight, value_weight, output_gate, beta_weight, decay_weight)
    piece_rows = lax.all_gather(mixer_in, "head", axis=0, tiled=True)
    projected = jnp.concatenate(
        [jnp.dot(piece_rows, matrix, preferred_element_type=jnp.float32) for matrix in weight_list],
        axis=1,
    )
    row_count = projected.shape[0]
    key_cols = query_weight.shape[1]
    value_cols = value_weight.shape[1]
    head_cols = beta_weight.shape[1]
    conv_cols = 2 * key_cols + value_cols
    qkv_raw = projected[:, :conv_cols].astype(jnp.bfloat16)
    gate_raw = projected[:, conv_cols : conv_cols + value_cols].astype(jnp.bfloat16)
    beta_raw = projected[:, conv_cols + value_cols : conv_cols + value_cols + head_cols]
    decay_raw = projected[:, conv_cols + value_cols + head_cols :]
    taps = jnp.concatenate([query_conv, key_conv, value_conv], axis=1)
    rim_len = taps.shape[0] - 1
    rim_cells = passed_along(qkv_raw[row_count - rim_len :], "ctx", 1)
    extended = jnp.concatenate([rim_cells.astype(jnp.float32), qkv_raw.astype(jnp.float32)], axis=0)
    summed = jnp.zeros((row_count, conv_cols), jnp.float32)
    for shift_index in range(rim_len + 1):
        summed = (
            summed + taps[shift_index][None, :] * extended[shift_index : shift_index + row_count]
        )
    convolved = jax.nn.silu(summed)
    key_width = DK
    key_heads = key_cols // key_width
    group_size = head_cols // key_heads
    queries = unit_heads(convolved[:, :key_cols], key_heads) * key_width ** (-0.5)
    key_rows = unit_heads(convolved[:, key_cols : 2 * key_cols], key_heads)
    values = convolved[:, 2 * key_cols :].reshape(row_count, head_cols, -1)
    strength = jax.nn.sigmoid(beta_raw)
    decays = -jnp.exp(decay_log)[None, :] * jax.nn.softplus(decay_raw + decay_bias[None, :])
    query_heads = jnp.repeat(queries, group_size, axis=1).transpose(1, 0, 2)
    key_head_rows = jnp.repeat(key_rows, group_size, axis=1).transpose(1, 0, 2)
    output_list, read_values, transfer, offset = jax.vmap(local_pass)(
        query_heads, key_head_rows, values.transpose(1, 0, 2), strength.T, decays.T
    )

    def compose(earlier, later):
        joined = jnp.einsum("hij,hjk->hik", later[0], earlier[0], precision=exact_precision)
        shifted = (
            jnp.einsum("hij,hjk->hik", later[0], earlier[1], precision=exact_precision) + later[1]
        )
        return (joined, shifted)

    identity = (
        jnp.broadcast_to(jnp.eye(transfer.shape[1], dtype=jnp.float32), transfer.shape),
        jnp.zeros_like(offset),
    )
    incoming_rows = prefix((transfer, offset), "ctx", compose, identity)[1]
    delta_core_output = output_list + jnp.einsum(
        "wnc,wcg->wng", read_values, incoming_rows, precision=exact_precision
    )
    delta_core_output = delta_core_output.transpose(1, 0, 2)
    normal = (
        delta_core_output
        * lax.rsqrt(
            jnp.mean(delta_core_output * delta_core_output, axis=-1, keepdims=True) + epsilon
        )
        * head_gain
    )
    gate_values = gate_raw.astype(jnp.float32).reshape(row_count, head_cols, -1)
    gated_out = (
        (normal * jax.nn.silu(gate_values)).astype(jnp.bfloat16).reshape(row_count, value_cols)
    )
    mixer_out = lax.psum_scatter(
        jnp.dot(gated_out, out_weight, preferred_element_type=jnp.float32).astype(jnp.bfloat16),
        "head",
        scatter_dimension=0,
        tiled=True,
    )
    return (moe_out, mixer_out)


def solution(mesh):
    return jax.shard_map(
        on_device,
        mesh=mesh,
        in_specs=(
            P(("ctx", "head"), None),
            P(),
            P(),
            P(("ctx", "head"), None),
            P(("ctx", "head"), None, None),
            P(("ctx", "head"), None, None),
            P(("ctx", "head"), None, None),
            P(),
            P(None, "head"),
            P(None, "head"),
            P(None, "head"),
            P(None, "head"),
            P(None, "head"),
            P(None, "head"),
            P(None, "head"),
            P(None, "head"),
            P(None, "head"),
            P("head"),
            P("head"),
            P(),
            P("head", None),
        ),
        out_specs=(P(("ctx", "head"), None), P(("ctx", "head"), None)),
        check_vma=False,
    )
```

profile of v0, /device:TPU:1, one launch (start us, length us, event | category | flops | bytes accessed | tf_op | source)
XLA Modules:
  0.0 852.3 jit_solution(13656351736903203024)
XLA Ops:
  17.1 34.2 %scatter_custom_fusion = bf16[1536,2048]{1,0:T(8,128)(2,1)} fusion(s32[1280]{0:T(1024)S(1)} %fusion.111, bf16[128,2048]{1,0:T(8,128)(2,1)S(1)} %fusion.102, s32[2048]{0:T(1024)S(1)} %pad_clamp_fusion.1, bf16[]{:T(256)} %constant.111.clone.1), kind=kCustom, calls=%fused_computation.65 | custom fusion | bytes 6291458 | tf_op jit(solution)/shard_map/scatter | solution.py:166
  51.3 11.0 %reshape.241 = bf16[128,2,6,2048]{3,2,1,0:T(8,128)(2,1)} reshape(bf16[1536,2048]{1,0:T(8,128)(2,1)} %scatter_custom_fusion) | data formatting | bytes 12582912 | tf_op jit(solution)/shard_map/reshape | solution.py:168
  62.3 9.6 %copy.131 = bf16[128,2,6,2048]{3,1,2,0:T(2,128)(2,1)S(1)} copy(bf16[128,2,6,2048]{3,2,1,0:T(8,128)(2,1)} %reshape.241) | data formatting | bytes 12582912 | tf_op jit(solution)/shard_map/reshape | solution.py:168
  72.0 87.2 %all_to_all.10 = bf16[128,2,6,2048]{3,1,2,0:T(2,128)(2,1)S(1)} all-to-all(bf16[128,2,6,2048]{3,1,2,0:T(2,128)(2,1)S(1)} %copy.131), channel_id=1, replica_groups=mesh['ctx'=32,'head'=4] {'ctx','head'}, dimensions={0} | all-to-all | bytes 12582912 | tf_op jit(solution)/shard_map/all_to_all | solution.py:169
  161.9 8.6 %fusion.48 = f32[2,128,6,512]{3,1,2,0:T(8,128)} fusion(bf16[128,2,6,2048]{3,1,2,0:T(2,128)(2,1)S(1)} %all_to_all.10, bf16[2,2048,512]{2,1,0:T(8,128)(2,1)S(1)} %copy-done.22), kind=kOutput, calls=%fused_computation.61 | convolution fusion | flops 3221225472 | bytes 13631488 | tf_op jit(solution)/shard_map/nesd,edh->nesh/dot_general | solution.py:173
  170.4 19.9 %convert_bitcast_fusion = bf16[128,2,6,2048]{3,0,2,1:T(8,128)(2,1)} fusion(bf16[2,512,2048]{2,1,0:T(8,128)(2,1)} %param.31, f32[2,128,6,512]{3,1,2,0:T(8,128)} %fusion.48, bf16[2,2048,512]{2,1,0:T(8,128)(2,1)} %param.29, bf16[128,2,6,2048]{3,1,2,0:T(2,128)(2,1)} %copy-done.7), kind=kOutput, calls=%fused_computation.60 | convolution fusion | flops 6450315264 | bytes 24117248 | tf_op jit(solution)/shard_map/nesh,ehd->nesd/dot_general | solution.py:176
  190.3 12.8 %copy.134 = bf16[128,2,6,2048]{3,1,2,0:T(2,128)(2,1)} copy(bf16[128,2,6,2048]{3,0,2,1:T(8,128)(2,1)} %convert_bitcast_fusion) | data formatting | bytes 12582912 | tf_op jit(solution)/shard_map/convert_element_type | solution.py:178
  203.1 4.9 all-to-all-start.1
  209.9 10.3 %gather_fusion.1 = f32[1280]{0:T(1024)S(1)} fusion(f32[128,256]{1,0:T(8,128)S(1)} %fusion.119, s32[1280]{0:T(1024)S(1)} %reshape.277), kind=kCustom, calls=%fused_computation.2 | custom fusion | bytes 20480 | tf_op jit(solution)/shard_map/jit(take_along_axis)/gather | solution.py:153
  220.6 64.5 %all-to-all-done.1 = bf16[128,2,6,2048]{3,1,2,0:T(2,128)(2,1)} async-done(((bf16[128,2,6,2048]{3,1,2,0:T(2,128)(2,1)}), bf16[128,2,6,2048]{3,1,2,0:T(2,128)(2,1)}, u32[]{:S(2)}, u32[]{:S(2)}) %all-to-all-start.1) | async-done | bytes 6291488 | tf_op jit(solution)/shard_map/all_to_all | solution.py:175
  285.0 10.4 %copy.135 = bf16[128,2,6,2048]{3,2,1,0:T(8,128)(2,1)} copy(bf16[128,2,6,2048]{3,1,2,0:T(2,128)(2,1)} %all-to-all-done.1) | data formatting | bytes 12582912 | tf_op jit(solution)/shard_map/all_to_all | solution.py:175
  295.4 11.0 %reshape.242 = bf16[1536,2048]{1,0:T(8,128)(2,1)} reshape(bf16[128,2,6,2048]{3,2,1,0:T(8,128)(2,1)} %copy.135) | data formatting | bytes 12582912 | tf_op jit(solution)/shard_map/reshape | solution.py:184
  306.5 14.4 %gather_fusion = bf16[1280,2048]{1,0:T(8,128)(2,1)} fusion(bf16[1536,2048]{1,0:T(8,128)(2,1)} %reshape.242, s32[2048]{0:T(1024)S(1)} %pad_clamp_fusion), kind=kCustom, calls=%fused_computation.1 | custom fusion | bytes 10490880 | tf_op jit(solution)/shard_map/gather | solution.py:184
  320.9 10.5 %reshape.258 = f32[128,10,2048]{2,1,0:T(8,128)} reshape(bf16[1280,2048]{1,0:T(8,128)(2,1)} %gather_fusion) | data formatting | bytes 15728640 | tf_op jit(solution)/shard_map/convert_element_type | solution.py:187
  331.4 9.6 %multiply_reduce_fusion = bf16[128,2048]{1,0:T(8,128)(2,1)S(1)} fusion(f32[128,10,2048]{2,1,0:T(8,128)} %reshape.258, f32[128,10]{1,0:T(8,128)S(1)} %copy.125), kind=kLoop, calls=%fused_computation.59 | loop fusion | flops 4980736 | bytes 11015168 | tf_op jit(solution)/shard_map/reduce_sum | solution.py:187
  343.9 27.1 %all-gather.6.cloned.1.call-done = bf16[512,2048]{1,0:T(8,128)(2,1)} async-done(((bf16[128,2048]{1,0:T(8,128)(2,1)}), bf16[512,2048]{1,0:T(8,128)(2,1)}) %all-gather.6.cloned.1.call-update) | async-done | bytes 2097168 | tf_op jit(solution)/shard_map/all_gather | solution.py:194
  387.5 6.4 divide_multiply_fusion
  403.0 158.7 %custom-call.4 = f32[4,8,1,64,64]{3,4,2,1,0:T(8,128)} custom-call(f32[4,8,1,64,64]{4,3,2,1,0:T(8,128)} %fusion.88), custom_call_target="InvertDiagBlocksLowerTriangular" | custom-call | tf_op jit(solution)/shard_map/vmap(vmap(jit(_solve_triangular)))/triangular_solve | solution.py:62
  573.3 100.6 %while.31 = (s32[]{:T(128)}, f32[4,128,128]{2,1,0:T(8,128)S(1)}, f32[4,128,128]{2,1,0:T(8,128)S(1)}, f32[8,4,64,128]{3,2,0,1:T(8,128)}, f32[8,4,64,128]{3,2,0,1:...) while((s32[]{:T(128)}, f32[4,128,128]{2,1,0:T(8,128)S(1)}, ...), condition=%wide.region_12.13_spmd.clone, body=%wide.region_11.12_spmd.clone.sunk | while | flops 352878592 | bytes 4855501 | solution.py:109
  675.7 4.3 convolution_convert_fusion.1
  681.6 39.2 %all-gather.8.cloned.1.call-done = bf16[128,128,128]{2,1,0:T(8,128)(2,1)} async-done(((bf16[4,128,128]{2,1,0:T(8,128)(2,1)}), bf16[128,128,128]{2,1,0:T(8,128)(2,1)}) %all-gather.8.cloned.1.call-update) | async-done | bytes 4194320 | tf_op jit(solution)/shard_map/all_gather | solution.py:21
  720.8 48.0 %all-gather.10.cloned.1.call-done = bf16[128,128,128]{2,1,0:T(8,128)(2,1)} async-done(((bf16[4,128,128]{2,1,0:T(8,128)(2,1)}), bf16[128,128,128]{2,1,0:T(8,128)(2,1)}) %all-gather.10.cloned.1.call-update) | async-done | bytes 4194320 | tf_op jit(solution)/shard_map/all_gather | solution.py:21
  768.8 42.3 %while.32 = (s32[]{:T(128)}, f32[4,128,128]{2,1,0:T(8,128)S(1)}, s32[]{:T(128)}, bf16[32,4,128,128]{3,2,1,0:T(8,128)(2,1)}, bf16[32,4,128,128]{3,2,1,0:T(8,128)(2,1)}, /*index=5*/s32[]{:T(128)}, s32[]{:T(128)}) while((s32[]{:T(128)}, f32[4,128,128]{2,1,0:T(8,128)S(1)}, s32[]{:T(128)}, bf16[32,4,128,128]{3,2,1,0:T(8,128)(2,1)}, ...), condition=%wide.region_14.15_spmd.clone, body=%wide.region_13.14_spmd.clone.sunk | while | flops 100990976 | bytes 1575519 | solution.py:38
  816.6 28.7 %reduce-scatter.2.cloned.1.call-done = bf16[128,2048]{1,0:T(8,128)(2,1)} async-done(((bf16[512,2048]{1,0:T(8,128)(2,1)}), bf16[128,2048]{1,0:T(8,128)(2,1)}) %reduce-scatter.2.cloned.1.call-update) | async-done | bytes 524304 | tf_op jit(solution)/shard_map/reduce_scatter | solution.py:259
  (282 shorter events, 204.5 us)
Async XLA Ops:
  7.2 806.8 %copy-start = (bf16[512,2048]{1,0:T(8,128)(2,1)S(1)}, bf16[512,2048]{1,0:T(8,128)(2,1)}, u32[]{:S(2)}) copy-start(bf16[512,2048]{1,0:T(8,128)(2,1)} %param.45) | copy-start | bytes 6291460
  12.8 2.1 copy-start.6
  12.8 4.1 copy-start.15
  72.0 89.9 %copy-start.22 = (bf16[2,2048,512]{2,1,0:T(8,128)(2,1)S(1)}, bf16[2,2048,512]{2,1,0:T(8,128)(2,1)}, u32[]{:S(2)}) copy-start(bf16[2,2048,512]{2,1,0:T(8,128)(2,1)} %param.30) | copy-start | bytes 12582916
  159.2 2.6 copy-start.7
  203.1 5.0 copy-start.12
  203.1 82.0 %all-to-all-start.1 = ((bf16[128,2,6,2048]{3,1,2,0:T(2,128)(2,1)}), bf16[128,2,6,2048]{3,1,2,0:T(2,128)(2,1)}, u32[]{:S(2)}, u32[]{:S(2)}) async-start(bf16[128,2,6,2048]{3,1,2,0:T(2,128)(2,1)} %copy.134), calls=%async_computation.1 | async-start | bytes 12582912 | tf_op jit(solution)/shard_map/all_to_all | solution.py:175
  208.0 162.9 %all-gather.6.cloned.1.call-start = ((), (), s32[]{:S(2)}) async-start(), calls=%async_computation.3 | async-start | bytes 2621440 | tf_op jit(solution)/shard_map/all_gather | solution.py:194
  331.4 9.9 %copy-start.16 = (f32[2048]{0:T(1024)S(1)}, f32[2048]{0:T(1024)}, u32[]{:S(2)}) copy-start(f32[2048]{0:T(1024)} %param.32) | copy-start | bytes 24580
  341.0 33.6 %copy-start.8 = (bf16[128,2048]{1,0:T(8,128)(2,1)}, bf16[128,2048]{1,0:T(8,128)(2,1)S(1)}, u32[]{:S(2)}) copy-start(bf16[128,2048]{1,0:T(8,128)(2,1)S(1)} %multiply_reduce_fusion) | copy-start | bytes 1572868
  341.0 2.1 copy-start.25
  342.4 378.5 %all-gather.8.cloned.1.call-start = ((), (), s32[]{:S(2)}) async-start(), calls=%async_computation.5 | async-start | bytes 4325376 | tf_op jit(solution)/shard_map/all_gather | solution.py:21
  370.9 3.7 copy-start.5
  370.9 3.7 copy-start.23
  376.6 5.6 copy-start.13
  376.7 5.6 copy-start.21
  378.4 6.0 copy-start.14
  378.5 8.9 %collective-permute-start = (bf16[3,1024]{0,1:T(8,128)(2,1)S(1)}, bf16[3,1024]{0,1:T(8,128)(2,1)S(1)}, u32[]{:S(2)}, u32[]{:S(2)}) collective-permute-start(bf16[3,1024]{0,1:T(8,128)(2,1)S(1)} %slice.81), channel_id=1, source_target_pairs={{0,4},{4,8},{8,12},{12,16},{16,20},{20,24},{24,28},{28,32},{32,36}... | collective-permute-start | bytes 18440 | tf_op jit(solution)/shard_map/ppermute | solution.py:15
  397.2 164.4 %slice-start = ((f32[512,1024]{0,1:T(8,128)}), f32[512,512]{0,1:T(8,128)S(1)}, s32[]{:S(2)}) async-start(f32[512,1024]{0,1:T(8,128)} %copy-done.1), calls=%async_computation.7 | async-start | bytes 2097152 | tf_op jit(solution)/shard_map/slice | solution.py:223
  564.3 2.2 copy-start.10
  674.6 94.2 %all-gather.10.cloned.1.call-start = ((), (), s32[]{:S(2)}) async-start(), calls=%async_computation.6 | async-start | bytes 4325376 | tf_op jit(solution)/shard_map/all_gather | solution.py:21
  675.3 170.0 %reduce-scatter.2.cloned.1.call-start = ((), (), s32[]{:S(2)}) async-start(), calls=%async_computation.4 | async-start | bytes 2621440 | tf_op jit(solution)/shard_map/reduce_scatter | solution.py:259
  811.1 2.4 copy-start.11
  811.1 2.4 copy-start.20
  (9 other events, 12.4 us)
Sparse Core Ops, SparseCore 0:
  342.5 28.4 all-gather.5
  674.7 46.0 all-gather.7
  723.1 45.6 all-gather.9
  816.7 28.5 reduce-scatter.1
where the time goes:
time: 859 us; the launch traced here: 852 us
  waiting for transfers between devices  208 us (24%)
  matrix products  191 us (22%)
  other arithmetic  189 us (22%)
  local copies, waits for them, and re-layouts  152 us (18%)
  blocking collectives  87.2 us (10%)
  between operations  14.9 us (2%)
  starting transfers between devices  9.12 us (1%)
    another operation x2, other arithmetic, block_terms(): jax.scipy.linalg.solve_triangular(system, targets, lower=True, unit_diago...  159 us
    all_to_all x1, blocking collectives, on_device(): lax.all_to_all(outgoing, ('ctx', 'head'), split_axis=0, concat_axis=0, ti...  87.2 us
    all_gather x2, waiting for transfers between devices, prefix(): lax.all_gather(part.astype(kind), axis)  87.2 us
    all_to_all x1, waiting for transfers between devices, on_device(): lax.all_to_all(jnp.einsum('nesh,ehd->nesd', hidden, expert_down, preferre...  64.5 us
    dot_general x32, matrix products, compose(): jnp.einsum('hij,hjk->hik', later[0], earlier[1], precision=exact_precision)  40.5 us
    scatter x1, local copies, waits for them, and re-layouts, on_device(): outgoing = jnp.zeros((experts_all * capacity, model_width), jnp.bfloat16)...  34.2 us
    reduce_scatter x1, waiting for transfers between devices, on_device(): lax.psum_scatter(jnp.dot(gated_out, out_weight, preferred_element_type=jn...  28.7 us
    all_gather x1, waiting for transfers between devices, on_device(): piece_rows = lax.all_gather(mixer_in, 'head', axis=0, tiled=True)  27.1 us
  transfers between devices with their start and end apart: 6, of which 5 were waited for; matrix products, arithmetic and copies ran while one was open for 3% of the time, Pallas kernels for 0%

commit v1 on v0

--- a/solution.py
+++ b/solution.py
@@ -191,7 +191,9 @@
         stream.astype(jnp.float32) + moe_out.astype(jnp.float32), mixer_gain
     ).astype(jnp.bfloat16)
     weight_list = (query_weight, key_weight, value_weight, output_gate, beta_weight, decay_weight)
-    piece_rows = lax.all_gather(mixer_in, "head", axis=0, tiled=True)
+    piece_rows = lax.all_to_all(
+        jnp.concatenate(lax.axis_size("head") * [mixer_in], axis=0), "head", 0, 0, tiled=True
+    )
     projected = jnp.concatenate(
         [jnp.dot(piece_rows, matrix, preferred_element_type=jnp.float32) for matrix in weight_list],
         axis=1,

time: 859 us -> 864 us (level)
    all_gather x1 -> x0, waiting for transfers between devices: 27.1 us -> none  [on_device(): piece_rows = lax.all_gather(mixer_in, 'head', axis=0, tiled=True)]
    all_to_all x0 -> x1, waiting for transfers between devices: none -> 24.2 us  [on_device(): lax.all_to_all(jnp.concatenate(lax.axis_size('head') * [mixer_in], axis=0...]
where the time goes in v1:
time: 864 us; the launch traced here: 857 us
  waiting for transfers between devices  204 us (24%)
  matrix products  196 us (23%)
  other arithmetic  190 us (22%)
  local copies, waits for them, and re-layouts  151 us (17%)
  blocking collectives  87.2 us (10%)
  between operations  14.9 us (2%)
  starting transfers between devices  12.7 us (1%)
    another operation x2, other arithmetic, block_terms(): jax.scipy.linalg.solve_triangular(system, targets, lower=True, unit_diago...  159 us
    all_to_all x1, blocking collectives, on_device(): lax.all_to_all(outgoing, ('ctx', 'head'), split_axis=0, concat_axis=0, ti...  87.2 us
    all_gather x2, waiting for transfers between devices, prefix(): lax.all_gather(part.astype(kind), axis)  86.5 us
    all_to_all x1, waiting for transfers between devices, on_device(): lax.all_to_all(jnp.einsum('nesh,ehd->nesd', hidden, expert_down, preferre...  64.3 us
    dot_general x32, matrix products, compose(): jnp.einsum('hij,hjk->hik', later[0], earlier[1], precision=exact_precision)  40.5 us
    scatter x1, local copies, waits for them, and re-layouts, on_device(): outgoing = jnp.zeros((experts_all * capacity, model_width), jnp.bfloat16)...  34.2 us
    reduce_scatter x1, waiting for transfers between devices, on_device(): lax.psum_scatter(jnp.dot(gated_out, out_weight, preferred_element_type=jn...  28.7 us
    all_to_all x1, waiting for transfers between devices, on_device(): lax.all_to_all(jnp.concatenate(lax.axis_size('head') * [mixer_in], axis=0...  24.2 us
  transfers between devices with their start and end apart: 6, of which 5 were waited for; matrix products, arithmetic and copies ran while one was open for 3% of the time, Pallas kernels for 0%

profile of v1, /device:TPU:1, one launch (start us, length us, event | category | flops | bytes accessed | tf_op | source)
XLA Modules:
  0.0 857.2 jit_solution(3957865146737101263)
XLA Ops:
  17.1 34.2 %scatter_custom_fusion = bf16[1536,2048]{1,0:T(8,128)(2,1)} fusion(s32[1280]{0:T(1024)S(1)} %fusion.111, bf16[128,2048]{1,0:T(8,128)(2,1)S(1)} %fusion.102, s32[2048]{0:T(1024)S(1)} %pad_clamp_fusion.1, bf16[]{:T(256)} %constant.111.clone.1), kind=kCustom, calls=%fused_computation.65 | custom fusion | bytes 6291458 | tf_op jit(solution)/shard_map/scatter | solution.py:166
  51.3 11.0 %reshape.243 = bf16[128,2,6,2048]{3,2,1,0:T(8,128)(2,1)} reshape(bf16[1536,2048]{1,0:T(8,128)(2,1)} %scatter_custom_fusion) | data formatting | bytes 12582912 | tf_op jit(solution)/shard_map/reshape | solution.py:168
  62.3 9.6 %copy.131 = bf16[128,2,6,2048]{3,1,2,0:T(2,128)(2,1)S(1)} copy(bf16[128,2,6,2048]{3,2,1,0:T(8,128)(2,1)} %reshape.243) | data formatting | bytes 12582912 | tf_op jit(solution)/shard_map/reshape | solution.py:168
  72.0 87.2 %all_to_all.22 = bf16[128,2,6,2048]{3,1,2,0:T(2,128)(2,1)S(1)} all-to-all(bf16[128,2,6,2048]{3,1,2,0:T(2,128)(2,1)S(1)} %copy.131), channel_id=1, replica_groups=mesh['ctx'=32,'head'=4] {'ctx','head'}, dimensions={0} | all-to-all | bytes 12582912 | tf_op jit(solution)/shard_map/all_to_all | solution.py:169
  161.8 8.6 %fusion.48 = f32[2,128,6,512]{3,1,2,0:T(8,128)} fusion(bf16[128,2,6,2048]{3,1,2,0:T(2,128)(2,1)S(1)} %all_to_all.22, bf16[2,2048,512]{2,1,0:T(8,128)(2,1)S(1)} %copy-done.21), kind=kOutput, calls=%fused_computation.61 | convolution fusion | flops 3221225472 | bytes 13631488 | tf_op jit(solution)/shard_map/nesd,edh->nesh/dot_general | solution.py:173
  170.4 19.9 %convert_bitcast_fusion = bf16[128,2,6,2048]{3,0,2,1:T(8,128)(2,1)} fusion(bf16[2,512,2048]{2,1,0:T(8,128)(2,1)} %param.31, f32[2,128,6,512]{3,1,2,0:T(8,128)} %fusion.48, bf16[2,2048,512]{2,1,0:T(8,128)(2,1)} %param.29, bf16[128,2,6,2048]{3,1,2,0:T(2,128)(2,1)} %copy-done.6), kind=kOutput, calls=%fused_computation.60 | convolution fusion | flops 6450315264 | bytes 24117248 | tf_op jit(solution)/shard_map/nesh,ehd->nesd/dot_general | solution.py:176
  190.3 12.7 %copy.134 = bf16[128,2,6,2048]{3,1,2,0:T(2,128)(2,1)} copy(bf16[128,2,6,2048]{3,0,2,1:T(8,128)(2,1)} %convert_bitcast_fusion) | data formatting | bytes 12582912 | tf_op jit(solution)/shard_map/convert_element_type | solution.py:178
  203.0 5.3 all-to-all-start.1
  210.1 10.1 %gather_fusion.1 = f32[1280]{0:T(1024)S(1)} fusion(f32[128,256]{1,0:T(8,128)S(1)} %fusion.119, s32[1280]{0:T(1024)S(1)} %reshape.279), kind=kCustom, calls=%fused_computation.2 | custom fusion | bytes 20480 | tf_op jit(solution)/shard_map/jit(take_along_axis)/gather | solution.py:153
  220.6 64.3 %all-to-all-done.1 = bf16[128,2,6,2048]{3,1,2,0:T(2,128)(2,1)} async-done(((bf16[128,2,6,2048]{3,1,2,0:T(2,128)(2,1)}), bf16[128,2,6,2048]{3,1,2,0:T(2,128)(2,1)}, u32[]{:S(2)}, u32[]{:S(2)}) %all-to-all-start.1) | async-done | bytes 6291488 | tf_op jit(solution)/shard_map/all_to_all | solution.py:175
  285.0 10.4 %copy.135 = bf16[128,2,6,2048]{3,2,1,0:T(8,128)(2,1)} copy(bf16[128,2,6,2048]{3,1,2,0:T(2,128)(2,1)} %all-to-all-done.1) | data formatting | bytes 12582912 | tf_op jit(solution)/shard_map/all_to_all | solution.py:175
  295.4 11.0 %reshape.244 = bf16[1536,2048]{1,0:T(8,128)(2,1)} reshape(bf16[128,2,6,2048]{3,2,1,0:T(8,128)(2,1)} %copy.135) | data formatting | bytes 12582912 | tf_op jit(solution)/shard_map/reshape | solution.py:184
  306.4 14.4 %gather_fusion = bf16[1280,2048]{1,0:T(8,128)(2,1)} fusion(bf16[1536,2048]{1,0:T(8,128)(2,1)} %reshape.244, s32[2048]{0:T(1024)S(1)} %pad_clamp_fusion), kind=kCustom, calls=%fused_computation.1 | custom fusion | bytes 10490880 | tf_op jit(solution)/shard_map/gather | solution.py:184
  320.8 10.5 %reshape.260 = f32[128,10,2048]{2,1,0:T(8,128)} reshape(bf16[1280,2048]{1,0:T(8,128)(2,1)} %gather_fusion) | data formatting | bytes 15728640 | tf_op jit(solution)/shard_map/convert_element_type | solution.py:187
  331.3 9.6 %multiply_reduce_fusion = bf16[128,2048]{1,0:T(8,128)(2,1)S(1)} fusion(f32[128,10,2048]{2,1,0:T(8,128)} %reshape.260, f32[128,10]{1,0:T(8,128)S(1)} %copy.125), kind=kLoop, calls=%fused_computation.59 | loop fusion | flops 4980736 | bytes 11015168 | tf_op jit(solution)/shard_map/reduce_sum | solution.py:187
  343.1 4.6 all-to-all-start.2
  349.3 24.2 %all-to-all-done.2 = bf16[4,128,2048]{2,1,0:T(8,128)(2,1)} async-done(((bf16[4,128,2048]{2,1,0:T(8,128)(2,1)}), bf16[4,128,2048]{2,1,0:T(8,128)(2,1)}, u32[]{:S(2)}, u32[]{:S(2)}) %all-to-all-start.2) | async-done | bytes 2097184 | tf_op jit(solution)/shard_map/all_to_all | solution.py:194
  393.0 6.5 divide_multiply_fusion
  408.6 158.7 %custom-call.4 = f32[4,8,1,64,64]{3,4,2,1,0:T(8,128)} custom-call(f32[4,8,1,64,64]{4,3,2,1,0:T(8,128)} %fusion.88), custom_call_target="InvertDiagBlocksLowerTriangular" | custom-call | tf_op jit(solution)/shard_map/vmap(vmap(jit(_solve_triangular)))/triangular_solve | solution.py:62
  578.9 100.5 %while.31 = (s32[]{:T(128)}, f32[4,128,128]{2,1,0:T(8,128)S(1)}, f32[4,128,128]{2,1,0:T(8,128)S(1)}, f32[8,4,64,128]{3,2,0,1:T(8,128)}, f32[8,4,64,128]{3,2,0,1:...) while((s32[]{:T(128)}, f32[4,128,128]{2,1,0:T(8,128)S(1)}, ...), condition=%wide.region_12.13_spmd.clone, body=%wide.region_11.12_spmd.clone.sunk | while | flops 352878592 | bytes 4855501 | solution.py:109
  687.1 38.6 %all-gather.5.cloned.1.call-done = bf16[128,128,128]{2,1,0:T(8,128)(2,1)} async-done(((bf16[4,128,128]{2,1,0:T(8,128)(2,1)}), bf16[128,128,128]{2,1,0:T(8,128)(2,1)}) %all-gather.5.cloned.1.call-update) | async-done | bytes 4194320 | tf_op jit(solution)/shard_map/all_gather | solution.py:21
  725.6 48.0 %all-gather.7.cloned.1.call-done = bf16[128,128,128]{2,1,0:T(8,128)(2,1)} async-done(((bf16[4,128,128]{2,1,0:T(8,128)(2,1)}), bf16[128,128,128]{2,1,0:T(8,128)(2,1)}) %all-gather.7.cloned.1.call-update) | async-done | bytes 4194320 | tf_op jit(solution)/shard_map/all_gather | solution.py:21
  773.6 42.3 %while.32 = (s32[]{:T(128)}, f32[4,128,128]{2,1,0:T(8,128)S(1)}, s32[]{:T(128)}, bf16[32,4,128,128]{3,2,1,0:T(8,128)(2,1)}, bf16[32,4,128,128]{3,2,1,0:T(8,128)(2,1)}, /*index=5*/s32[]{:T(128)}, s32[]{:T(128)}) while((s32[]{:T(128)}, f32[4,128,128]{2,1,0:T(8,128)S(1)}, s32[]{:T(128)}, bf16[32,4,128,128]{3,2,1,0:T(8,128)(2,1)}, ...), condition=%wide.region_14.15_spmd.clone, body=%wide.region_13.14_spmd.clone.sunk | while | flops 100990976 | bytes 1575519 | solution.py:38
  821.5 28.7 %reduce-scatter.2.cloned.1.call-done = bf16[128,2048]{1,0:T(8,128)(2,1)} async-done(((bf16[512,2048]{1,0:T(8,128)(2,1)}), bf16[128,2048]{1,0:T(8,128)(2,1)}) %reduce-scatter.2.cloned.1.call-update) | async-done | bytes 524304 | tf_op jit(solution)/shard_map/reduce_scatter | solution.py:261
  (280 shorter events, 212.6 us)
Async XLA Ops:
  7.2 811.6 %copy-start = (bf16[512,2048]{1,0:T(8,128)(2,1)S(1)}, bf16[512,2048]{1,0:T(8,128)(2,1)}, u32[]{:S(2)}) copy-start(bf16[512,2048]{1,0:T(8,128)(2,1)} %param.45) | copy-start | bytes 6291460
  12.8 4.1 copy-start.14
  71.9 89.9 %copy-start.21 = (bf16[2,2048,512]{2,1,0:T(8,128)(2,1)S(1)}, bf16[2,2048,512]{2,1,0:T(8,128)(2,1)}, u32[]{:S(2)}) copy-start(bf16[2,2048,512]{2,1,0:T(8,128)(2,1)} %param.30) | copy-start | bytes 12582916
  159.2 2.6 copy-start.6
  203.0 5.3 copy-start.11
  203.0 81.9 %all-to-all-start.1 = ((bf16[128,2,6,2048]{3,1,2,0:T(2,128)(2,1)}), bf16[128,2,6,2048]{3,1,2,0:T(2,128)(2,1)}, u32[]{:S(2)}, u32[]{:S(2)}) async-start(bf16[128,2,6,2048]{3,1,2,0:T(2,128)(2,1)} %copy.134), calls=%async_computation.1 | async-start | bytes 12582912 | tf_op jit(solution)/shard_map/all_to_all | solution.py:175
  331.3 9.9 %copy-start.15 = (f32[2048]{0:T(1024)S(1)}, f32[2048]{0:T(1024)}, u32[]{:S(2)}) copy-start(f32[2048]{0:T(1024)} %param.32) | copy-start | bytes 24580
  343.1 4.7 copy-start.17
  343.1 4.8 copy-start.18
  343.1 4.8 copy-start.16
  343.1 5.5 copy-start.24
  343.1 30.4 %all-to-all-start.2 = ((bf16[4,128,2048]{2,1,0:T(8,128)(2,1)}), bf16[4,128,2048]{2,1,0:T(8,128)(2,1)}, u32[]{:S(2)}, u32[]{:S(2)}) async-start(bf16[4,128,2048]{2,1,0:T(8,128)(2,1)} %bitcast.246), calls=%async_computation.2 | async-start | bytes 4194304 | tf_op jit(solution)/shard_map/all_to_all | solution.py:194
  347.7 377.9 %all-gather.5.cloned.1.call-start = ((), (), s32[]{:S(2)}) async-start(), calls=%async_computation.5 | async-start | bytes 4325376 | tf_op jit(solution)/shard_map/all_gather | solution.py:21
  373.5 3.6 copy-start.22
  377.1 2.5 copy-start.23
  381.9 4.3 copy-start.12
  381.9 4.2 copy-start.20
  383.6 4.9 copy-start.13
  383.8 9.2 %collective-permute-start = (bf16[3,1024]{0,1:T(8,128)(2,1)S(1)}, bf16[3,1024]{0,1:T(8,128)(2,1)S(1)}, u32[]{:S(2)}, u32[]{:S(2)}) collective-permute-start(bf16[3,1024]{0,1:T(8,128)(2,1)S(1)} %slice.81), channel_id=1, source_target_pairs={{0,4},{4,8},{8,12},{12,16},{16,20},{20,24},{24,28},{28,32},{32,36}... | collective-permute-start | bytes 18440 | tf_op jit(solution)/shard_map/ppermute | solution.py:15
  402.8 164.4 %slice-start = ((f32[512,1024]{0,1:T(8,128)}), f32[512,512]{0,1:T(8,128)S(1)}, s32[]{:S(2)}) async-start(f32[512,1024]{0,1:T(8,128)} %copy-done.1), calls=%async_computation.7 | async-start | bytes 2097152 | tf_op jit(solution)/shard_map/slice | solution.py:225
  680.1 93.5 %all-gather.7.cloned.1.call-start = ((), (), s32[]{:S(2)}) async-start(), calls=%async_computation.6 | async-start | bytes 4325376 | tf_op jit(solution)/shard_map/all_gather | solution.py:21
  680.9 169.3 %reduce-scatter.2.cloned.1.call-start = ((), (), s32[]{:S(2)}) async-start(), calls=%async_computation.4 | async-start | bytes 2621440 | tf_op jit(solution)/shard_map/reduce_scatter | solution.py:261
  815.9 2.4 copy-start.10
  815.9 2.4 copy-start.19
  (8 other events, 13.2 us)
Sparse Core Ops, SparseCore 0:
  680.2 45.3 all-gather.4
  727.9 45.6 all-gather.6
  821.6 28.5 reduce-scatter.1
